TPU v7x, 256 devices: a whole 4x4x8 slice. The times are simulated.
256 devices in a mesh: tm: 32 (over z, x), fsdp: 8 (over y, core).
Axes of the slice: x: 4, y: 4, z: 8, core: 2. Of those that a mesh axis runs over, the one named last changes fastest.
Arguments:
- frames: bfloat16 [64, 64, 256, 128], P('tm', None, 'fsdp'), may hold values from -6 to 6
- conv_weight: bfloat16 [3, 3, 3, 128, 128], P(None, None, None, None, 'fsdp'), may hold values from -0.109375 to 0.109375
- mix_weight: bfloat16 [3, 128, 128], P(None, None, 'fsdp'), may hold values from -0.3125 to 0.3125
- cotangent: bfloat16 [32, 64, 256, 128], P(None, 'tm', 'fsdp'), may hold values from -0.008239746 to 0.008239746
Outputs:
- encoded: bfloat16 [32, 64, 256, 128], P(None, 'tm', 'fsdp')
- mix_grad: float32 [49152], P(('tm', 'fsdp'))
All inputs are finite; a program needn't handle non-finite values.
Results may differ from a plain program's by a relative error of at most 0.0058.
Values may be sent and summed in bfloat16 or wider, within the bound.
A program may use at most 64 MiB of HBM per device.

v0:
```python
import jax
import jax.numpy as jnp
from jax import lax
from jax.sharding import PartitionSpec as P


def from_behind(block, axis, distance):
    devices = range(lax.axis_size(axis))
    route = [(i - distance, i) for i in devices if i - distance in devices]
    return lax.ppermute(block, axis, route)


def with_halo(cells, sides, width):
    for axis, dim in sides:
        count = lax.axis_size(axis)
        ends = count - 1
        head = lax.slice_in_dim(cells, 0, width, axis=dim)
        tail = lax.slice_in_dim(cells, cells.shape[dim] - width, cells.shape[dim], axis=dim)
        cells = jnp.concatenate(
            [
                lax.ppermute(tail, axis, [(i, (i + 1) % count) for i in range(ends)]),
                cells,
                lax.ppermute(head, axis, [((i + 1) % count, i) for i in range(ends)]),
            ],
            axis=dim,
        )
    return cells


def pool_pairs(hidden):
    shaped = hidden.reshape((hidden.shape[0] // 2, 2) + hidden.shape[1:]).astype(jnp.float32)
    return ((shaped[:, 0] + shaped[:, 1]) * 0.5).astype(jnp.bfloat16)


def delayed(block, offset):
    return jnp.pad(block, ((offset, 0), (0, 0), (0, 0), (0, 0)))[: block.shape[0]]


def local(frames, conv_weight, mix_weight, cotangent):
    full_conv, full_mix = (
        lax.all_gather(conv_weight, "fsdp", axis=4, tiled=True),
        lax.all_gather(mix_weight, "fsdp", axis=2, tiled=True),
    )
    count_frames, height, width, channels = frames.shape
    previous = from_behind(frames, "tm", 1)
    timed = jnp.concatenate([previous, frames], axis=0)
    padded = with_halo(timed, (("fsdp", 2),), 1)
    padded = jnp.pad(padded, ((0, 0), (1, 1), (0, 0), (0, 0)))
    accum = jnp.zeros((count_frames * height * width, channels), jnp.float32)
    for row_tap in range(3):
        for col_tap in range(3):
            stacked = jnp.concatenate(
                [
                    padded[
                        step : step + count_frames,
                        row_tap : row_tap + height,
                        col_tap : col_tap + width,
                        :,
                    ]
                    for step in range(3)
                ],
                axis=3,
            ).reshape(-1, 3 * channels)
            kernel = full_conv[:, row_tap, col_tap].reshape(3 * channels, channels)
            accum = accum + jnp.dot(stacked, kernel, preferred_element_type=jnp.float32)
    hidden = jax.nn.silu(accum).astype(jnp.bfloat16).reshape(count_frames, height, width, channels)
    pooled = lax.all_to_all(pool_pairs(hidden), "tm", split_axis=1, concat_axis=0, tiled=True)
    branch = pooled.astype(jnp.float32).reshape(-1, channels)
    flat_cot = cotangent.reshape(-1, channels)
    grad_terms = []
    for offset in range(3):
        lagged = delayed(pooled, offset).reshape(-1, channels)
        branch = branch + jnp.dot(lagged, full_mix[offset], preferred_element_type=jnp.float32)
        grad_terms.append(
            lax.dot_general(
                lagged, flat_cot, (((0,), (0,)), ((), ())), preferred_element_type=jnp.float32
            )
        )
    encoded = branch.astype(jnp.bfloat16).reshape(pooled.shape)
    parts = lax.axis_size("tm") * lax.axis_size("fsdp")
    mix_grad = lax.all_to_all(
        jnp.stack(grad_terms).reshape(parts, -1), ("tm", "fsdp"), 0, 0, tiled=True
    ).sum(0)
    return (encoded, mix_grad)


def solution(mesh):
    return jax.shard_map(
        local,
        mesh=mesh,
        in_specs=(
            P("tm", None, "fsdp", None),
            P(None, None, None, None, "fsdp"),
            P(None, None, "fsdp"),
            P(None, "tm", "fsdp", None),
        ),
        out_specs=(P(None, "tm", "fsdp", None), P(("tm", "fsdp"))),
        check_vma=False,
    )
```

profile of v0, /device:TPU:1, one launch (start us, length us, event | category | flops | bytes accessed | tf_op | source)
XLA Modules:
  0.0 129.5 jit_solution(5271844698895392121)
XLA Ops:
  0.7 4.1 %collective-permute-start = (bf16[2,64,32,128]{3,2,1,0:T(8,128)(2,1)}, bf16[2,64,32,128]{3,2,1,0:T(8,128)(2,1)S(1)}, u32[]{:S(2)}, u32[]{:S(2)}) collective-permute-start(bf16[2,64,32,128]{3,2,1,0:T(8,128)(2,1)} %param.4), channel_id=1, source_target_pairs={{0,8},{8,16},{16,24},{24,32},{32,40},{40,48},{48,56},{56,64},{64,7... | collective-permute-start | bytes 3145736 | tf_op jit(solution)/shard_map/ppermute | solution.py:10
  4.8 15.0 %all_gather.6 = bf16[3,3,3,128,128]{3,4,2,1,0:T(8,128)(2,1)S(1)} all-gather(bf16[3,3,3,128,16]{3,4,2,1,0:T(8,128)(2,1)} %param.5), channel_id=1, replica_groups=mesh['tm'=32,'fsdp'=8] {'fsdp'}, dimensions={4}, use_global_device_ids=true | all-gather | bytes 995328 | tf_op jit(solution)/shard_map/all_gather | solution.py:41
  19.8 7.0 %collective-permute-done = bf16[2,64,32,128]{3,2,1,0:T(8,128)(2,1)S(1)} collective-permute-done((bf16[2,64,32,128]{3,2,1,0:T(8,128)(2,1)}, bf16[2,64,32,128]{3,2,1,0:T(8,128)(2,1)S(1)}, u32[]{:S(2)}, u32[]{:S(2)}) %collective-permute-start) | collective-permute-done | bytes 1048608 | tf_op jit(solution)/shard_map/ppermute | solution.py:10
  28.0 3.4 %collective-permute-start.2 = (bf16[4,64,1,128]{3,2,1,0:T(2,128)(2,1)}, bf16[4,64,1,128]{3,2,1,0:T(2,128)(2,1)S(1)}, u32[]{:S(2)}, u32[]{:S(2)}) collective-permute-start(bf16[4,64,1,128]{3,2,1,0:T(2,128)(2,1)} %get-tuple-element.30), channel_id=1, source_target_pairs={{1,0},{2,1},{3,2},{4,3},{5,4},{6,5},{7,6},{9,8},{10,9},{11,10},{12... | collective-permute-start | bytes 196616 | tf_op jit(solution)/shard_map/ppermute | solution.py:23
  31.5 3.1 %collective-permute-start.1 = (bf16[4,64,1,128]{3,2,1,0:T(2,128)(2,1)}, bf16[4,64,1,128]{3,2,1,0:T(2,128)(2,1)S(1)}, u32[]{:S(2)}, u32[]{:S(2)}) collective-permute-start(bf16[4,64,1,128]{3,2,1,0:T(2,128)(2,1)} %get-tuple-element.29), channel_id=1, source_target_pairs={{0,1},{1,2},{2,3},{3,4},{4,5},{5,6},{6,7},{8,9},{9,10},{10,11},{11... | collective-permute-start | bytes 196616 | tf_op jit(solution)/shard_map/ppermute | solution.py:21
  35.3 1.6 %copy.19 = bf16[3,1,1,128,128]{4,3,0,2,1:T(8,128)(2,1)} copy(bf16[3,1,1,128,128]{3,4,2,1,0:T(8,128)(2,1)} %get-tuple-element.39) | data formatting | bytes 196608
  39.4 1.6 %copy.27 = bf16[3,1,1,128,128]{4,3,0,2,1:T(8,128)(2,1)} copy(bf16[3,1,1,128,128]{3,4,2,1,0:T(8,128)(2,1)} %get-tuple-element.31) | data formatting | bytes 196608
  41.1 1.5 %fusion.7 = bf16[4,66,34,128]{3,2,1,0:T(8,128)(2,1)S(1)} fusion(bf16[4,64,1,128]{3,2,1,0:T(2,128)(2,1)S(1)} %collective-permute-done.2, bf16[4,64,32,128]{3,2,1,0:T(8,128)(2,1)S(1)} %constant_dynamic-update-slice_fusion, bf16[4,64,1,128]{3,2,1,0:T(2,128)(2,1)S(1)} %collective-permute-done.1), kind=kLoop, calls=%fused_computation.30 | loop fusion | flops 13787136 | bytes 4526080 | tf_op jit(solution)/shard_map/concatenate | solution.py:19
  42.6 6.9 %fusion.16 = (bf16[2,64,32,128]{3,2,1,0:T(8,128)(2,1)S(1)}, bf16[2,64,32,128]{3,2,1,0:T(8,128)(2,1)S(1)}, bf16[2,64,32,128]{3,2,1,0:T(8,128)(2,1)S(1)}, bf16[2,6...) fusion(bf16[4,66,34,128]{3,2,1,0:T(8,128)(2,1)S(1)} %fusion.7), kind=kLoop, calls=%fused_computation.59 | loop fusion | bytes 37748736 | tf_op jit(solution)/shard_map/slice | solution.py:54
  49.5 3.3 %pad_maximum_fusion.2 = (bf16[2,64,32,384]{3,2,1,0:T(8,128)(2,1)S(1)}, bf16[2,64,32,384]{3,2,1,0:T(8,128)(2,1)S(1)}) fusion(bf16[2,64,32,128]{3,2,1,0:T(8,128)(2,1)} %get-tuple-element.16, bf16[2,64,32,128]{3,2,1,0:T(8,128)(2,1)} %get-tuple-element.17, bf16[2,64,32,128]{3,2,1,0:T(8,128)(2,1)} %get-tuple-element.18, ...), kind=kLoop, calls=%fused_computation.19 | loop fusion | flops 18874368 | bytes 12582912 | tf_op jit(solution)/shard_map/concatenate | solution.py:52
  53.9 1.1 convolution_add_fusion.7
  57.8 2.1 %fusion.10 = (bf16[2,64,32,128]{3,2,1,0:T(8,128)(2,1)S(1)}, bf16[2,64,32,128]{3,2,1,0:T(8,128)(2,1)S(1)}, bf16[2,64,32,128]{3,2,1,0:T(8,128)(2,1)S(1)}, bf16[2,6...) fusion(bf16[4,64,32,128]{3,2,1,0:T(8,128)(2,1)S(1)} %constant_dynamic-update-slice_fusion, ...), kind=kLoop, calls=%fused_computation.44 | loop fusion | flops 8388608 | bytes 8650752 | tf_op jit(solution)/shard_map/concatenate | solution.py:19
  60.0 2.5 %fusion.1 = (bf16[2,64,32,384]{3,2,1,0:T(8,128)(2,1)S(1)}, bf16[2,64,32,384]{3,2,1,0:T(8,128)(2,1)S(1)}) fusion(bf16[4,64,1,128]{3,2,1,0:T(2,128)(2,1)S(1)} %collective-permute-done.2, bf16[4,64,32,128]{3,2,1,0:T(8,128)(2,1)S(1)} %constant_dynamic-update-slice_fusion, bf16[2,64,32,128]{3,2,1,0:T(8,128)(2,1)S(1)} %get-tuple-element.21, ...), kind=kLoop, calls=%fused_computation.16 | loop fusion | flops 25165824 | bytes 12713984 | tf_op jit(solution)/shard_map/concatenate | solution.py:52
  66.5 1.0 convolution_add_fusion.2
  68.4 1.0 convolution_add_fusion.1
  69.5 1.1 multiply_convert_fusion
  70.9 1.0 fusion.15
  71.9 12.8 %all-to-all-start = ((bf16[1,64,32,128]{3,2,0,1:T(8,128)(2,1)}), bf16[1,64,32,128]{3,2,0,1:T(8,128)(2,1)S(1)}, u32[]{:S(2)}, u32[]{:S(2)}) async-start(bf16[1,64,32,128]{3,2,0,1:T(8,128)(2,1)} %fusion.15), calls=%async_computation | async-start | bytes 1048576 | tf_op jit(solution)/shard_map/all_to_all | solution.py:67
  84.8 12.7 %all_gather.7 = bf16[3,128,128]{1,2,0:T(8,128)(2,1)S(1)} all-gather(bf16[3,128,16]{1,2,0:T(8,128)(2,1)S(1)} %copy-done.12), channel_id=1, replica_groups=mesh['tm'=32,'fsdp'=8] {'fsdp'}, dimensions={2}, use_global_device_ids=true | all-gather | bytes 110592 | tf_op jit(solution)/shard_map/all_gather | solution.py:42
  97.4 4.7 %all-to-all-done = bf16[1,64,32,128]{3,2,0,1:T(8,128)(2,1)S(1)} async-done(((bf16[1,64,32,128]{3,2,0,1:T(8,128)(2,1)}), bf16[1,64,32,128]{3,2,0,1:T(8,128)(2,1)S(1)}, u32[]{:S(2)}, u32[]{:S(2)}) %all-to-all-start) | async-done | bytes 524320 | tf_op jit(solution)/shard_map/all_to_all | solution.py:67
  103.7 1.1 all_to_all.22
  104.9 8.5 %all-to-all-start.1 = ((f32[256,1,192]{2,1,0:T(1,128)}), f32[256,1,192]{2,1,0:T(1,128)S(1)}, u32[]{:S(2)}, u32[]{:S(2)}) async-start(f32[256,1,192]{2,1,0:T(1,128)} %all_to_all.22), calls=%async_computation.1 | async-start | bytes 524288 | tf_op jit(solution)/shard_map/all_to_all | solution.py:81
  113.7 1.1 fusion.8
  114.8 13.9 %all-to-all-done.1 = f32[256,1,192]{2,1,0:T(1,128)S(1)} async-done(((f32[256,1,192]{2,1,0:T(1,128)}), f32[256,1,192]{2,1,0:T(1,128)S(1)}, u32[]{:S(2)}, u32[]{:S(2)}) %all-to-all-start.1) | async-done | bytes 196640 | tf_op jit(solution)/shard_map/all_to_all | solution.py:81
  (56 shorter events, 16.0 us)
Async XLA Ops:
  0.6 101.7 %copy-start = (bf16[32,2,32,128]{3,2,1,0:T(8,128)(2,1)S(1)}, bf16[32,2,32,128]{3,2,1,0:T(8,128)(2,1)}, u32[]{:S(2)}) copy-start(bf16[32,2,32,128]{3,2,1,0:T(8,128)(2,1)} %param.7) | copy-start | bytes 1572868
  0.6 26.3 %copy-start.5 = (bf16[2,64,32,128]{3,2,1,0:T(8,128)(2,1)S(1)}, bf16[2,64,32,128]{3,2,1,0:T(8,128)(2,1)}, u32[]{:S(2)}) copy-start(bf16[2,64,32,128]{3,2,1,0:T(8,128)(2,1)} %param.4) | copy-start | bytes 3145732
  0.7 26.2 %collective-permute-start = (bf16[2,64,32,128]{3,2,1,0:T(8,128)(2,1)}, bf16[2,64,32,128]{3,2,1,0:T(8,128)(2,1)S(1)}, u32[]{:S(2)}, u32[]{:S(2)}) collective-permute-start(bf16[2,64,32,128]{3,2,1,0:T(8,128)(2,1)} %param.4), channel_id=1, source_target_pairs={{0,8},{8,16},{16,24},{24,32},{32,40},{40,48},{48,56},{56,64},{64,7... | collective-permute-start | bytes 3145736 | tf_op jit(solution)/shard_map/ppermute | solution.py:10
  26.9 8.5 %copy-start.7 = (bf16[2,64,32,128]{3,2,1,0:T(8,128)(2,1)}, bf16[2,64,32,128]{3,2,1,0:T(8,128)(2,1)S(1)}, u32[]{:S(2)}) copy-start(bf16[2,64,32,128]{3,2,1,0:T(8,128)(2,1)S(1)} %collective-permute-done) | copy-start | bytes 3145732
  28.0 13.0 %collective-permute-start.2 = (bf16[4,64,1,128]{3,2,1,0:T(2,128)(2,1)}, bf16[4,64,1,128]{3,2,1,0:T(2,128)(2,1)S(1)}, u32[]{:S(2)}, u32[]{:S(2)}) collective-permute-start(bf16[4,64,1,128]{3,2,1,0:T(2,128)(2,1)} %get-tuple-element.30), channel_id=1, source_target_pairs={{1,0},{2,1},{3,2},{4,3},{5,4},{6,5},{7,6},{9,8},{10,9},{11,10},{12... | collective-permute-start | bytes 196616 | tf_op jit(solution)/shard_map/ppermute | solution.py:23
  31.5 9.6 %collective-permute-start.1 = (bf16[4,64,1,128]{3,2,1,0:T(2,128)(2,1)}, bf16[4,64,1,128]{3,2,1,0:T(2,128)(2,1)S(1)}, u32[]{:S(2)}, u32[]{:S(2)}) collective-permute-start(bf16[4,64,1,128]{3,2,1,0:T(2,128)(2,1)} %get-tuple-element.29), channel_id=1, source_target_pairs={{0,1},{1,2},{2,3},{3,4},{4,5},{5,6},{6,7},{8,9},{9,10},{10,11},{11... | collective-permute-start | bytes 196616 | tf_op jit(solution)/shard_map/ppermute | solution.py:21
  49.5 3.3 %copy-start.10 = (bf16[3,1,1,128,128]{4,3,0,2,1:T(8,128)(2,1)S(1)}, bf16[3,1,1,128,128]{4,3,0,2,1:T(8,128)(2,1)}, u32[]{:S(2)}) copy-start(bf16[3,1,1,128,128]{4,3,0,2,1:T(8,128)(2,1)} %copy.19) | copy-start | bytes 294916
  52.8 1.0 copy-start.9
  53.8 1.2 copy-start.1
  53.8 1.5 %copy-start.2 = (bf16[2,64,32,128]{3,2,1,0:T(8,128)(2,1)S(1)}, bf16[2,64,32,128]{3,2,1,0:T(8,128)(2,1)}, u32[]{:S(2)}) copy-start(bf16[2,64,32,128]{3,2,1,0:T(8,128)(2,1)} %get-tuple-element.10) | copy-start | bytes 3145732
  53.8 1.8 %copy-start.3 = (bf16[2,64,32,128]{3,2,1,0:T(8,128)(2,1)S(1)}, bf16[2,64,32,128]{3,2,1,0:T(8,128)(2,1)}, u32[]{:S(2)}) copy-start(bf16[2,64,32,128]{3,2,1,0:T(8,128)(2,1)} %get-tuple-element.11) | copy-start | bytes 3145732
  53.8 2.1 %copy-start.4 = (bf16[2,64,32,128]{3,2,1,0:T(8,128)(2,1)S(1)}, bf16[2,64,32,128]{3,2,1,0:T(8,128)(2,1)}, u32[]{:S(2)}) copy-start(bf16[2,64,32,128]{3,2,1,0:T(8,128)(2,1)} %get-tuple-element.12) | copy-start | bytes 3145732
  62.5 1.2 copy-start.6
  62.5 1.5 %copy-start.8 = (bf16[2,64,32,128]{3,2,1,0:T(8,128)(2,1)S(1)}, bf16[2,64,32,128]{3,2,1,0:T(8,128)(2,1)}, u32[]{:S(2)}) copy-start(bf16[2,64,32,128]{3,2,1,0:T(8,128)(2,1)} %copy-done.7) | copy-start | bytes 3145732
  68.4 1.0 copy-start.11
  70.6 14.1 %copy-start.12 = (bf16[3,128,16]{1,2,0:T(8,128)(2,1)S(1)}, bf16[3,128,16]{1,2,0:T(8,128)(2,1)}, u32[]{:S(2)}) copy-start(bf16[3,128,16]{1,2,0:T(8,128)(2,1)} %param.6) | copy-start | bytes 36868
  71.9 30.2 %all-to-all-start = ((bf16[1,64,32,128]{3,2,0,1:T(8,128)(2,1)}), bf16[1,64,32,128]{3,2,0,1:T(8,128)(2,1)S(1)}, u32[]{:S(2)}, u32[]{:S(2)}) async-start(bf16[1,64,32,128]{3,2,0,1:T(8,128)(2,1)} %fusion.15), calls=%async_computation | async-start | bytes 1048576 | tf_op jit(solution)/shard_map/all_to_all | solution.py:67
  104.9 23.8 %all-to-all-start.1 = ((f32[256,1,192]{2,1,0:T(1,128)}), f32[256,1,192]{2,1,0:T(1,128)S(1)}, u32[]{:S(2)}, u32[]{:S(2)}) async-start(f32[256,1,192]{2,1,0:T(1,128)} %all_to_all.22), calls=%async_computation.1 | async-start | bytes 524288 | tf_op jit(solution)/shard_map/all_to_all | solution.py:81
where the time goes:
time: 130 us
  starting transfers between devices  32 us (25%)
  blocking collectives  27.7 us (21%)
  waiting for transfers between devices  25.6 us (20%)
  local copies, waits for them, and re-layouts  17.5 us (13%)
  other arithmetic  13.8 us (11%)
  matrix products  11.9 us (9%)
    all_gather x1, blocking collectives, local(): lax.all_gather(conv_weight, 'fsdp', axis=4, tiled=True)  15 us
    all_to_all x1, waiting for transfers between devices, local(): lax.all_to_all(jnp.stack(grad_terms).reshape(parts, -1), ('tm', 'fsdp'),...  13.9 us
    all_to_all x1, starting transfers between devices, local(): lax.all_to_all(pool_pairs(hidden), 'tm', split_axis=1, concat_axis=0, til...  12.8 us
    all_gather x1, blocking collectives, local(): lax.all_gather(mix_weight, 'fsdp', axis=2, tiled=True)  12.7 us
    dot_general x9, matrix products, local(): accum = accum + jnp.dot(stacked, kernel, preferred_element_type=jnp.float32)  9.18 us
    all_to_all x1, starting transfers between devices, local(): lax.all_to_all(jnp.stack(grad_terms).reshape(parts, -1), ('tm', 'fsdp'),...  8.54 us
    concatenate x5, other arithmetic, local(): jnp.concatenate([padded[step:step + count_frames, row_tap:row_tap + heigh...  7.93 us
    unnamed x36, local copies, waits for them, and re-layouts  7.4 us
  transfers between devices with their start and end apart: 5, of which 3 were waited for; matrix products, arithmetic and copies ran while one was open for 6% of the time, Pallas kernels for 0%

commit v1 on v0

--- a/solution.py
+++ b/solution.py
@@ -38,7 +38,9 @@
 
 def local(frames, conv_weight, mix_weight, cotangent):
     full_conv, full_mix = (
-        lax.all_gather(conv_weight, "fsdp", axis=4, tiled=True),
+        jnp.concatenate(
+            lax.all_to_all(jnp.stack([conv_weight] * lax.axis_size("fsdp")), "fsdp", 0, 0), axis=4
+        ),
         lax.all_gather(mix_weight, "fsdp", axis=2, tiled=True),
     )
     count_frames, height, width, channels = frames.shape

time: 130 us -> 130 us (level)
  waiting for transfers between devices: 25.6 us -> 20.6 us
  blocking collectives: 27.7 us -> 31.4 us
  local copies, waits for them, and re-layouts: 17.5 us -> 18.8 us
    all_to_all x0 -> x1, blocking collectives: none -> 18.7 us  [local(): lax.all_to_all(jnp.stack([conv_weight] * lax.axis_size('fsdp')), 'fsdp',...]
    all_gather x1 -> x0, blocking collectives: 15 us -> none  [local(): lax.all_gather(conv_weight, 'fsdp', axis=4, tiled=True)]
    slice x1 -> x10, local copies, waits for them, and re-layouts: 0.76 us -> 6.43 us  [local(): kernel = full_conv[:, row_tap, col_tap].reshape(3 * channels, channels)]
    unnamed x36 -> x27, local copies, waits for them, and re-layouts: 7.4 us -> 1.73 us
    ppermute x1, waiting for transfers between devices: 7.05 us -> 2.09 us  [from_behind(): return lax.ppermute(block, axis, route)]
  transfers between devices with their start and end apart: 5 -> 5, of which waited for: 3 -> 3; matrix products, arithmetic and copies ran while one was open for 6% -> 7% of each run, Pallas kernels for 0% -> 0%
where the time goes in v1:
time: 130 us
  starting transfers between devices  32 us (25%)
  blocking collectives  31.4 us (24%)
  waiting for transfers between devices  20.6 us (16%)
  local copies, waits for them, and re-layouts  18.8 us (14%)
  other arithmetic  13.8 us (11%)
  matrix products  11.9 us (9%)
    all_to_all x1, blocking collectives, local(): lax.all_to_all(jnp.stack([conv_weight] * lax.axis_size('fsdp')), 'fsdp',...  18.7 us
    all_to_all x1, waiting for transfers between devices, local(): lax.all_to_all(jnp.stack(grad_terms).reshape(parts, -1), ('tm', 'fsdp'),...  13.9 us
    all_to_all x1, starting transfers between devices, local(): lax.all_to_all(pool_pairs(hidden), 'tm', split_axis=1, concat_axis=0, til...  12.8 us
    all_gather x1, blocking collectives, local(): lax.all_gather(mix_weight, 'fsdp', axis=2, tiled=True)  12.7 us
    dot_general x9, matrix products, local(): accum = accum + jnp.dot(stacked, kernel, preferred_element_type=jnp.float32)  9.18 us
    all_to_all x1, starting transfers between devices, local(): lax.all_to_all(jnp.stack(grad_terms).reshape(parts, -1), ('tm', 'fsdp'),...  8.54 us
    concatenate x5, other arithmetic, local(): jnp.concatenate([padded[step:step + count_frames, row_tap:row_tap + heigh...  7.93 us
    slice x1, local copies, waits for them, and re-layouts, local(): padded[step:step + count_frames, row_tap:row_tap + height, col_tap:col_ta...  6.92 us
  transfers between devices with their start and end apart: 5, of which 3 were waited for; matrix products, arithmetic and copies ran while one was open for 7% of the time, Pallas kernels for 0%

profile of v1, /device:TPU:1, one launch (start us, length us, event | category | flops | bytes accessed | tf_op | source)
XLA Modules:
  0.0 129.5 jit_solution(9501929181668379913)
XLA Ops:
  0.7 4.1 %collective-permute-start = (bf16[2,64,32,128]{3,2,1,0:T(8,128)(2,1)}, bf16[2,64,32,128]{3,2,1,0:T(8,128)(2,1)S(1)}, u32[]{:S(2)}, u32[]{:S(2)}) collective-permute-start(bf16[2,64,32,128]{3,2,1,0:T(8,128)(2,1)} %param.4), channel_id=1, source_target_pairs={{0,8},{8,16},{16,24},{24,32},{32,40},{40,48},{48,56},{56,64},{64,7... | collective-permute-start | bytes 3145736 | tf_op jit(solution)/shard_map/ppermute | solution.py:10
  5.8 18.7 %all_to_all.30 = bf16[8,3,3,3,128,16]{4,5,3,2,1,0:T(8,128)(2,1)S(1)} all-to-all(bf16[8,3,3,3,128,16]{4,5,3,2,1,0:T(8,128)(2,1)S(1)} %stack.10), channel_id=1, replica_groups=mesh['tm'=32,'fsdp'=8] {'fsdp'}, dimensions={0} | all-to-all | bytes 1769472 | tf_op jit(solution)/shard_map/all_to_all | solution.py:42
  24.8 2.1 %collective-permute-done = bf16[2,64,32,128]{3,2,1,0:T(8,128)(2,1)S(1)} collective-permute-done((bf16[2,64,32,128]{3,2,1,0:T(8,128)(2,1)}, bf16[2,64,32,128]{3,2,1,0:T(8,128)(2,1)S(1)}, u32[]{:S(2)}, u32[]{:S(2)}) %collective-permute-start) | collective-permute-done | bytes 1048608 | tf_op jit(solution)/shard_map/ppermute | solution.py:10
  28.0 3.4 %collective-permute-start.2 = (bf16[4,64,1,128]{3,2,1,0:T(2,128)(2,1)}, bf16[4,64,1,128]{3,2,1,0:T(2,128)(2,1)S(1)}, u32[]{:S(2)}, u32[]{:S(2)}) collective-permute-start(bf16[4,64,1,128]{3,2,1,0:T(2,128)(2,1)} %get-tuple-element.30), channel_id=1, source_target_pairs={{1,0},{2,1},{3,2},{4,3},{5,4},{6,5},{7,6},{9,8},{10,9},{11,10},{12... | collective-permute-start | bytes 196616 | tf_op jit(solution)/shard_map/ppermute | solution.py:23
  31.5 3.1 %collective-permute-start.1 = (bf16[4,64,1,128]{3,2,1,0:T(2,128)(2,1)}, bf16[4,64,1,128]{3,2,1,0:T(2,128)(2,1)S(1)}, u32[]{:S(2)}, u32[]{:S(2)}) collective-permute-start(bf16[4,64,1,128]{3,2,1,0:T(2,128)(2,1)} %get-tuple-element.29), channel_id=1, source_target_pairs={{0,1},{1,2},{2,3},{3,4},{4,5},{5,6},{6,7},{8,9},{9,10},{10,11},{11... | collective-permute-start | bytes 196616 | tf_op jit(solution)/shard_map/ppermute | solution.py:21
  35.3 1.6 %copy.17 = bf16[3,1,1,128,128]{4,3,0,2,1:T(8,128)(2,1)} copy(bf16[3,1,1,128,128]{3,4,2,1,0:T(8,128)(2,1)} %get-tuple-element.39) | data formatting | bytes 196608 | tf_op jit(solution)/shard_map/slice | solution.py:66
  39.4 1.6 %copy.25 = bf16[3,1,1,128,128]{4,3,0,2,1:T(8,128)(2,1)} copy(bf16[3,1,1,128,128]{3,4,2,1,0:T(8,128)(2,1)} %get-tuple-element.31) | data formatting | bytes 196608 | tf_op jit(solution)/shard_map/slice | solution.py:66
  41.1 1.5 %fusion.7 = bf16[4,66,34,128]{3,2,1,0:T(8,128)(2,1)S(1)} fusion(bf16[4,64,1,128]{3,2,1,0:T(2,128)(2,1)S(1)} %collective-permute-done.2, bf16[4,64,32,128]{3,2,1,0:T(8,128)(2,1)S(1)} %constant_dynamic-update-slice_fusion, bf16[4,64,1,128]{3,2,1,0:T(2,128)(2,1)S(1)} %collective-permute-done.1), kind=kLoop, calls=%fused_computation.30 | loop fusion | flops 13787136 | bytes 4526080 | tf_op jit(solution)/shard_map/concatenate | solution.py:19
  42.6 6.9 %fusion.16 = (bf16[2,64,32,128]{3,2,1,0:T(8,128)(2,1)S(1)}, bf16[2,64,32,128]{3,2,1,0:T(8,128)(2,1)S(1)}, bf16[2,64,32,128]{3,2,1,0:T(8,128)(2,1)S(1)}, bf16[2,6...) fusion(bf16[4,66,34,128]{3,2,1,0:T(8,128)(2,1)S(1)} %fusion.7), kind=kLoop, calls=%fused_computation.59 | loop fusion | bytes 37748736 | tf_op jit(solution)/shard_map/slice | solution.py:56
  49.5 3.3 %pad_maximum_fusion.2 = (bf16[2,64,32,384]{3,2,1,0:T(8,128)(2,1)S(1)}, bf16[2,64,32,384]{3,2,1,0:T(8,128)(2,1)S(1)}) fusion(bf16[2,64,32,128]{3,2,1,0:T(8,128)(2,1)} %get-tuple-element.16, bf16[2,64,32,128]{3,2,1,0:T(8,128)(2,1)} %get-tuple-element.17, bf16[2,64,32,128]{3,2,1,0:T(8,128)(2,1)} %get-tuple-element.18, ...), kind=kLoop, calls=%fused_computation.19 | loop fusion | flops 18874368 | bytes 12582912 | tf_op jit(solution)/shard_map/concatenate | solution.py:54
  53.9 1.1 convolution_add_fusion.7
  57.8 2.1 %fusion.10 = (bf16[2,64,32,128]{3,2,1,0:T(8,128)(2,1)S(1)}, bf16[2,64,32,128]{3,2,1,0:T(8,128)(2,1)S(1)}, bf16[2,64,32,128]{3,2,1,0:T(8,128)(2,1)S(1)}, bf16[2,6...) fusion(bf16[4,64,32,128]{3,2,1,0:T(8,128)(2,1)S(1)} %constant_dynamic-update-slice_fusion, ...), kind=kLoop, calls=%fused_computation.44 | loop fusion | flops 8388608 | bytes 8650752 | tf_op jit(solution)/shard_map/concatenate | solution.py:19
  60.0 2.5 %fusion.1 = (bf16[2,64,32,384]{3,2,1,0:T(8,128)(2,1)S(1)}, bf16[2,64,32,384]{3,2,1,0:T(8,128)(2,1)S(1)}) fusion(bf16[4,64,1,128]{3,2,1,0:T(2,128)(2,1)S(1)} %collective-permute-done.2, bf16[4,64,32,128]{3,2,1,0:T(8,128)(2,1)S(1)} %constant_dynamic-update-slice_fusion, bf16[2,64,32,128]{3,2,1,0:T(8,128)(2,1)S(1)} %get-tuple-element.21, ...), kind=kLoop, calls=%fused_computation.16 | loop fusion | flops 25165824 | bytes 12713984 | tf_op jit(solution)/shard_map/concatenate | solution.py:54
  66.5 1.0 convolution_add_fusion.2
  68.4 1.0 convolution_add_fusion.1
  69.5 1.1 multiply_convert_fusion
  70.9 1.0 fusion.15
  71.9 12.8 %all-to-all-start.1 = ((bf16[1,64,32,128]{3,2,0,1:T(8,128)(2,1)}), bf16[1,64,32,128]{3,2,0,1:T(8,128)(2,1)S(1)}, u32[]{:S(2)}, u32[]{:S(2)}) async-start(bf16[1,64,32,128]{3,2,0,1:T(8,128)(2,1)} %fusion.15), calls=%async_computation.1 | async-start | bytes 1048576 | tf_op jit(solution)/shard_map/all_to_all | solution.py:69
  84.8 12.7 %all_gather.3 = bf16[3,128,128]{1,2,0:T(8,128)(2,1)S(1)} all-gather(bf16[3,128,16]{1,2,0:T(8,128)(2,1)S(1)} %copy-done.12), channel_id=1, replica_groups=mesh['tm'=32,'fsdp'=8] {'fsdp'}, dimensions={2}, use_global_device_ids=true | all-gather | bytes 110592 | tf_op jit(solution)/shard_map/all_gather | solution.py:44
  97.4 4.7 %all-to-all-done.1 = bf16[1,64,32,128]{3,2,0,1:T(8,128)(2,1)S(1)} async-done(((bf16[1,64,32,128]{3,2,0,1:T(8,128)(2,1)}), bf16[1,64,32,128]{3,2,0,1:T(8,128)(2,1)S(1)}, u32[]{:S(2)}, u32[]{:S(2)}) %all-to-all-start.1) | async-done | bytes 524320 | tf_op jit(solution)/shard_map/all_to_all | solution.py:69
  103.7 1.1 all_to_all.26
  104.9 8.5 %all-to-all-start.2 = ((f32[256,1,192]{2,1,0:T(1,128)}), f32[256,1,192]{2,1,0:T(1,128)S(1)}, u32[]{:S(2)}, u32[]{:S(2)}) async-start(f32[256,1,192]{2,1,0:T(1,128)} %all_to_all.26), calls=%async_computation.2 | async-start | bytes 524288 | tf_op jit(solution)/shard_map/all_to_all | solution.py:83
  113.7 1.1 fusion.8
  114.8 13.9 %all-to-all-done.2 = f32[256,1,192]{2,1,0:T(1,128)S(1)} async-done(((f32[256,1,192]{2,1,0:T(1,128)}), f32[256,1,192]{2,1,0:T(1,128)S(1)}, u32[]{:S(2)}, u32[]{:S(2)}) %all-to-all-start.2) | async-done | bytes 196640 | tf_op jit(solution)/shard_map/all_to_all | solution.py:83
  (58 shorter events, 17.3 us)
Async XLA Ops:
  0.6 101.7 %copy-start = (bf16[32,2,32,128]{3,2,1,0:T(8,128)(2,1)S(1)}, bf16[32,2,32,128]{3,2,1,0:T(8,128)(2,1)}, u32[]{:S(2)}) copy-start(bf16[32,2,32,128]{3,2,1,0:T(8,128)(2,1)} %param.7) | copy-start | bytes 1572868
  0.6 26.3 %copy-start.5 = (bf16[2,64,32,128]{3,2,1,0:T(8,128)(2,1)S(1)}, bf16[2,64,32,128]{3,2,1,0:T(8,128)(2,1)}, u32[]{:S(2)}) copy-start(bf16[2,64,32,128]{3,2,1,0:T(8,128)(2,1)} %param.4) | copy-start | bytes 3145732
  0.7 26.2 %collective-permute-start = (bf16[2,64,32,128]{3,2,1,0:T(8,128)(2,1)}, bf16[2,64,32,128]{3,2,1,0:T(8,128)(2,1)S(1)}, u32[]{:S(2)}, u32[]{:S(2)}) collective-permute-start(bf16[2,64,32,128]{3,2,1,0:T(8,128)(2,1)} %param.4), channel_id=1, source_target_pairs={{0,8},{8,16},{16,24},{24,32},{32,40},{40,48},{48,56},{56,64},{64,7... | collective-permute-start | bytes 3145736 | tf_op jit(solution)/shard_map/ppermute | solution.py:10
  26.9 8.5 %copy-start.7 = (bf16[2,64,32,128]{3,2,1,0:T(8,128)(2,1)}, bf16[2,64,32,128]{3,2,1,0:T(8,128)(2,1)S(1)}, u32[]{:S(2)}) copy-start(bf16[2,64,32,128]{3,2,1,0:T(8,128)(2,1)S(1)} %collective-permute-done) | copy-start | bytes 3145732
  28.0 13.0 %collective-permute-start.2 = (bf16[4,64,1,128]{3,2,1,0:T(2,128)(2,1)}, bf16[4,64,1,128]{3,2,1,0:T(2,128)(2,1)S(1)}, u32[]{:S(2)}, u32[]{:S(2)}) collective-permute-start(bf16[4,64,1,128]{3,2,1,0:T(2,128)(2,1)} %get-tuple-element.30), channel_id=1, source_target_pairs={{1,0},{2,1},{3,2},{4,3},{5,4},{6,5},{7,6},{9,8},{10,9},{11,10},{12... | collective-permute-start | bytes 196616 | tf_op jit(solution)/shard_map/ppermute | solution.py:23
  31.5 9.6 %collective-permute-start.1 = (bf16[4,64,1,128]{3,2,1,0:T(2,128)(2,1)}, bf16[4,64,1,128]{3,2,1,0:T(2,128)(2,1)S(1)}, u32[]{:S(2)}, u32[]{:S(2)}) collective-permute-start(bf16[4,64,1,128]{3,2,1,0:T(2,128)(2,1)} %get-tuple-element.29), channel_id=1, source_target_pairs={{0,1},{1,2},{2,3},{3,4},{4,5},{5,6},{6,7},{8,9},{9,10},{10,11},{11... | collective-permute-start | bytes 196616 | tf_op jit(solution)/shard_map/ppermute | solution.py:21
  49.5 3.3 %copy-start.10 = (bf16[3,1,1,128,128]{4,3,0,2,1:T(8,128)(2,1)S(1)}, bf16[3,1,1,128,128]{4,3,0,2,1:T(8,128)(2,1)}, u32[]{:S(2)}) copy-start(bf16[3,1,1,128,128]{4,3,0,2,1:T(8,128)(2,1)} %copy.17) | copy-start | bytes 294916
  52.8 1.0 copy-start.9
  53.8 1.2 copy-start.1
  53.8 1.5 %copy-start.2 = (bf16[2,64,32,128]{3,2,1,0:T(8,128)(2,1)S(1)}, bf16[2,64,32,128]{3,2,1,0:T(8,128)(2,1)}, u32[]{:S(2)}) copy-start(bf16[2,64,32,128]{3,2,1,0:T(8,128)(2,1)} %get-tuple-element.10) | copy-start | bytes 3145732
  53.8 1.8 %copy-start.3 = (bf16[2,64,32,128]{3,2,1,0:T(8,128)(2,1)S(1)}, bf16[2,64,32,128]{3,2,1,0:T(8,128)(2,1)}, u32[]{:S(2)}) copy-start(bf16[2,64,32,128]{3,2,1,0:T(8,128)(2,1)} %get-tuple-element.11) | copy-start | bytes 3145732
  53.8 2.1 %copy-start.4 = (bf16[2,64,32,128]{3,2,1,0:T(8,128)(2,1)S(1)}, bf16[2,64,32,128]{3,2,1,0:T(8,128)(2,1)}, u32[]{:S(2)}) copy-start(bf16[2,64,32,128]{3,2,1,0:T(8,128)(2,1)} %get-tuple-element.12) | copy-start | bytes 3145732
  62.5 1.2 copy-start.6
  62.5 1.5 %copy-start.8 = (bf16[2,64,32,128]{3,2,1,0:T(8,128)(2,1)S(1)}, bf16[2,64,32,128]{3,2,1,0:T(8,128)(2,1)}, u32[]{:S(2)}) copy-start(bf16[2,64,32,128]{3,2,1,0:T(8,128)(2,1)} %copy-done.7) | copy-start | bytes 3145732
  68.4 1.0 copy-start.11
  70.6 14.1 %copy-start.12 = (bf16[3,128,16]{1,2,0:T(8,128)(2,1)S(1)}, bf16[3,128,16]{1,2,0:T(8,128)(2,1)}, u32[]{:S(2)}) copy-start(bf16[3,128,16]{1,2,0:T(8,128)(2,1)} %param.6) | copy-start | bytes 36868
  71.9 30.2 %all-to-all-start.1 = ((bf16[1,64,32,128]{3,2,0,1:T(8,128)(2,1)}), bf16[1,64,32,128]{3,2,0,1:T(8,128)(2,1)S(1)}, u32[]{:S(2)}, u32[]{:S(2)}) async-start(bf16[1,64,32,128]{3,2,0,1:T(8,128)(2,1)} %fusion.15), calls=%async_computation.1 | async-start | bytes 1048576 | tf_op jit(solution)/shard_map/all_to_all | solution.py:69
  104.9 23.8 %all-to-all-start.2 = ((f32[256,1,192]{2,1,0:T(1,128)}), f32[256,1,192]{2,1,0:T(1,128)S(1)}, u32[]{:S(2)}, u32[]{:S(2)}) async-start(f32[256,1,192]{2,1,0:T(1,128)} %all_to_all.26), calls=%async_computation.2 | async-start | bytes 524288 | tf_op jit(solution)/shard_map/all_to_all | solution.py:83
